TPU v7x, 32 devices: a whole 2x2x4 slice. The times are simulated.
32 devices in a mesh: row: 4 (over y, x), col: 8 (over z, core).
Axes of the slice: x: 2, y: 2, z: 4, core: 2. Of those that a mesh axis runs over, the one named last changes fastest.
Arguments:
- vectors: float32 [32, 32768], P(None, ('row', 'col'))
- tiles: float32 [4096, 128, 128], P(('row', 'col'))
- tile_row: int32 [32, 128], P(('row', 'col')), may hold values from 0 to 63, never falling along the last dimension, each value on 1 to 6 neighbouring positions
- tile_col: int32 [32, 128], P(('row', 'col')), may hold values from 0 to 31
Outputs:
- filtered: float32 [32, 32768], P(None, ('row', 'col'))
- gram: float32 [32, 32], replicated
Inputs may be any that keep to these rules, and one draw needn't show every extreme that they name: `tile_row`: on each device the entries never fall along the last dimension, and each of the 64 values is taken by 1 to 6 slots.
All inputs are finite; a program needn't handle non-finite values.
Results may differ from a plain program's by a relative error of at most 0.00015.
Values sent between devices are 32-bit elements; how exact they have to be, the bound alone decides.
No kernel may reach another device: no remote copies, remote signals or barrier semaphores. Data moves between devices by JAX's collectives and lax.ppermute only.
A program may use at most 64 MiB of HBM per device.

v0:
```python
import jax
import jax.numpy as jnp
from jax import lax
from jax.sharding import PartitionSpec as P

TB = 128
K = 32
STEPS = 3


def on_device(vectors, tiles, tile_row, tile_col):
    rows_here = tile_row[0]
    cols_here = tile_col[0]
    n_row = lax.axis_size("row")
    n_col = lax.axis_size("col")
    width = vectors.shape[1]
    owned = width // TB
    local_rows = n_col * owned
    local_cols = n_row * owned
    onehot = (rows_here[:, None] == jnp.arange(local_rows, dtype=jnp.int32)[None, :]).astype(
        jnp.float32
    )
    magnitude = jnp.sum(jnp.abs(tiles), axis=2)
    row_terms = jnp.einsum("ti,tl->li", magnitude, onehot, precision=lax.Precision.HIGHEST).reshape(
        local_rows * TB
    )
    degree = 1.0 + lax.psum_scatter(row_terms, "col", scatter_dimension=0, tiled=True)
    scale = 1.0 / jnp.sqrt(degree)

    def operate(current):
        scaled = current * scale[None, :]
        panel = lax.all_gather(scaled, "row", axis=1, tiled=True)
        picked = jnp.take(panel.reshape(K, local_cols, TB), cols_here, axis=1)
        product = jnp.einsum("tij,ktj->kti", tiles, picked, precision=lax.Precision.HIGHEST)
        partial_value = jnp.einsum(
            "kti,tl->kli", product, onehot, precision=lax.Precision.HIGHEST
        ).reshape(K, local_rows * TB)
        mine = lax.psum_scatter(partial_value, "col", scatter_dimension=1, tiled=True)
        return mine * scale[None, :]

    previous = vectors
    current = operate(vectors)
    for step in range(STEPS - 1):
        following = 2.0 * operate(current) - previous
        previous = current
        current = following
    local_gram = jnp.dot(current, current.T, precision=lax.Precision.HIGHEST)
    gram = lax.psum(local_gram, ("row", "col")) / (width * n_row * n_col)
    return (current, gram)


def solution(mesh):
    in_specs = (
        P(None, ("row", "col")),
        P(("row", "col"), None, None),
        P(("row", "col"), None),
        P(("row", "col"), None),
    )
    out_specs = (P(None, ("row", "col")), P())
    return jax.shard_map(
        on_device, mesh=mesh, in_specs=in_specs, out_specs=out_specs, check_vma=False
    )
```

profile of v0, /device:TPU:10, one launch (start us, length us, event | category | flops | bytes accessed | tf_op | source)
XLA Modules:
  0.0 275.3 jit_solution(16175437541620134693)
XLA Ops:
  8.6 5.7 %abs_reduce_fusion = f32[128,128]{1,0:T(8,128)S(1)} fusion(f32[128,128,128]{2,1,0:T(8,128)} %param.7), kind=kLoop, calls=%fused_computation.3 | loop fusion | flops 4177920 | bytes 8454144 | tf_op jit(solution)/shard_map/reduce_sum | solution.py:23
  14.4 25.2 %all-reduce = f32[8192]{0:T(1024)S(1)} all-reduce(f32[8192]{0:T(1024)S(1)} %convolution_bitcast_fusion), channel_id=2, replica_groups=mesh['row'=4,'col'=8] {'col'}, use_global_device_ids=true, to_apply=%region_1.0.clone | all-reduce | flops 8192 | bytes 65536
  40.9 10.1 %all_gather.9 = f32[32,4096]{1,0:T(8,128)S(1)} all-gather(f32[32,1024]{1,0:T(8,128)S(1)} %broadcast_multiply_fusion), channel_id=1, replica_groups=mesh['row'=4,'col'=8] {'row'}, dimensions={1}, use_global_device_ids=true | all-gather | bytes 655360 | tf_op jit(solution)/shard_map/all_gather | solution.py:32
  51.0 0.8 gather_fusion
  51.8 15.5 %fusion.15 = f32[32,128,128]{2,0,1:T(8,128)S(1)} fusion(f32[128,128,128]{2,1,0:T(8,128)} %param.7, f32[128,32,128]{2,1,0:T(8,128)S(1)} %gather_fusion, pred[128]{0:T(512)(128)(4,1)S(1)} %compare_and_fusion), kind=kOutput, calls=%fused_computation.19 | convolution fusion | flops 805830656 | bytes 12583040 | tf_op jit(solution)/shard_map/tij,ktj->kti/dot_general | solution.py:34
  67.3 2.1 fusion.10
  69.4 1.6 copy.38
  71.1 29.3 %reduce-scatter.4.cloned.1.call-done = f32[32,1024]{1,0:T(8,128)} async-done(((f32[32,8192]{1,0:T(8,128)}), f32[32,1024]{1,0:T(8,128)}) %reduce-scatter.4.cloned.1.call-update) | async-done | bytes 131088 | tf_op jit(solution)/shard_map/reduce_scatter | solution.py:38
  100.4 0.9 multiply_multiply_fusion
  101.3 10.5 %all_gather.10 = f32[32,4096]{1,0:T(8,128)S(1)} all-gather(f32[32,1024]{1,0:T(8,128)S(1)} %multiply_multiply_fusion), channel_id=1, replica_groups=mesh['row'=4,'col'=8] {'row'}, dimensions={1}, use_global_device_ids=true | all-gather | bytes 655360 | tf_op jit(solution)/shard_map/all_gather | solution.py:32
  111.8 0.8 gather_fusion.1
  112.6 15.5 %fusion.18 = f32[32,128,128]{2,0,1:T(8,128)S(1)} fusion(f32[128,128,128]{2,1,0:T(8,128)} %param.7, f32[128,32,128]{2,1,0:T(8,128)S(1)} %gather_fusion.1, pred[128]{0:T(512)(128)(4,1)S(1)} %compare_and_fusion), kind=kOutput, calls=%fused_computation.20 | convolution fusion | flops 805830656 | bytes 12583040 | tf_op jit(solution)/shard_map/tij,ktj->kti/dot_general | solution.py:34
  128.1 2.1 fusion.8
  130.2 1.6 copy.37
  131.9 30.1 %reduce-scatter.6.cloned.1.call-done = f32[32,1024]{1,0:T(8,128)} async-done(((f32[32,8192]{1,0:T(8,128)}), f32[32,1024]{1,0:T(8,128)}) %reduce-scatter.6.cloned.1.call-update) | async-done | bytes 131088 | tf_op jit(solution)/shard_map/reduce_scatter | solution.py:38
  162.0 0.9 subtract_multiply_fusion
  162.9 9.8 %all_gather.11 = f32[32,4096]{1,0:T(8,128)S(1)} all-gather(f32[32,1024]{1,0:T(8,128)S(1)} %subtract_multiply_fusion), channel_id=1, replica_groups=mesh['row'=4,'col'=8] {'row'}, dimensions={1}, use_global_device_ids=true | all-gather | bytes 655360 | tf_op jit(solution)/shard_map/all_gather | solution.py:32
  172.8 0.8 gather_fusion.2
  173.6 15.5 %fusion.21 = f32[32,128,128]{2,0,1:T(8,128)S(1)} fusion(f32[128,128,128]{2,1,0:T(8,128)} %param.7, f32[128,32,128]{2,1,0:T(8,128)S(1)} %gather_fusion.2, pred[128]{0:T(512)(128)(4,1)S(1)} %compare_and_fusion), kind=kOutput, calls=%fused_computation.21 | convolution fusion | flops 805830656 | bytes 12583040 | tf_op jit(solution)/shard_map/tij,ktj->kti/dot_general | solution.py:34
  189.1 2.1 fusion.6
  191.2 1.6 copy.36
  192.8 30.6 %reduce-scatter.8.cloned.1.call-done = f32[32,1024]{1,0:T(8,128)} async-done(((f32[32,8192]{1,0:T(8,128)}), f32[32,1024]{1,0:T(8,128)}) %reduce-scatter.8.cloned.1.call-update) | async-done | bytes 131088 | tf_op jit(solution)/shard_map/reduce_scatter | solution.py:38
  223.4 0.9 multiply_subtract_fusion
  224.6 43.5 %psum.7 = f32[32,32]{1,0:T(8,128)S(1)} all-reduce(f32[32,32]{1,0:T(8,128)S(1)} %fusion.42), channel_id=1, replica_groups=mesh['row'=4,'col'=8] {'row','col'}, use_global_device_ids=true, to_apply=%region_5.7 | all-reduce | flops 1024 | bytes 8192 | tf_op jit(solution)/shard_map/psum | solution.py:48
  (28 shorter events, 3.3 us)
Async XLA Ops:
  7.2 93.2 %reduce-scatter.4.cloned.1.call-start = ((), (), s32[]{:S(2)}) async-start(), calls=%async_computation.3 | async-start | bytes 1179648 | tf_op jit(solution)/shard_map/reduce_scatter | solution.py:38
  8.5 5.7 %copy-start.3 = (s32[1,128]{1,0:T(1,128)S(1)}, s32[1,128]{1,0:T(1,128)}, u32[]{:S(2)}) copy-start(s32[1,128]{1,0:T(1,128)} %param.8) | copy-start | bytes 1540
  8.6 31.1 %copy-start.4 = (u32[32]{0:T(128)S(1)}, u32[32]{0:T(128)}, u32[]{:S(2)}) copy-start(u32[32]{0:T(128)} %constant.23) | copy-start | bytes 388
  8.6 32.3 %copy-start.1 = (f32[32,1024]{1,0:T(8,128)S(1)}, f32[32,1024]{1,0:T(8,128)}, u32[]{:S(2)}) copy-start(f32[32,1024]{1,0:T(8,128)} %param.6) | copy-start | bytes 393220
  71.0 91.0 %reduce-scatter.6.cloned.1.call-start = ((), (), s32[]{:S(2)}) async-start(), calls=%async_computation.4 | async-start | bytes 1179648 | tf_op jit(solution)/shard_map/reduce_scatter | solution.py:38
  131.8 91.6 %reduce-scatter.8.cloned.1.call-start = ((), (), s32[]{:S(2)}) async-start(), calls=%async_computation.5 | async-start | bytes 1179648 | tf_op jit(solution)/shard_map/reduce_scatter | solution.py:38
  191.2 32.2 %copy-start.2 = (f32[32,1024]{1,0:T(8,128)S(1)}, f32[32,1024]{1,0:T(8,128)}, u32[]{:S(2)}) copy-start(f32[32,1024]{1,0:T(8,128)} %reduce-scatter.4.cloned.1.call-done) | copy-start | bytes 393220
  224.3 44.4 %copy-start = (f32[32,1024]{1,0:T(8,128)}, f32[32,1024]{1,0:T(8,128)S(1)}, u32[]{:S(2)}) copy-start(f32[32,1024]{1,0:T(8,128)S(1)} %multiply_subtract_fusion) | copy-start | bytes 393220
Sparse Core Ops, SparseCore 0:
  71.2 29.1 reduce-scatter.3
  132.0 30.0 reduce-scatter.5
  192.9 30.4 reduce-scatter.7
where the time goes:
time: 276 us; the launch traced here: 275 us
  blocking collectives  99 us (36%)
  waiting for transfers between devices  90.1 us (33%)
  matrix products  53.1 us (19%)
  between operations  14.6 us (5%)
  other arithmetic  10.4 us (4%)
  local copies, waits for them, and re-layouts  7.97 us (3%)
    reduce_scatter x3, waiting for transfers between devices, operate(): lax.psum_scatter(partial_value, 'col', scatter_dimension=1, tiled=True)  90 us
    dot_general x3, matrix products, operate(): jnp.einsum('tij,ktj->kti', tiles, picked, precision=lax.Precision.HIGHEST)  46.4 us
    psum x1, blocking collectives, on_device(): gram = lax.psum(local_gram, ('row', 'col')) / (width * n_row * n_col)  43.5 us
    all_gather x3, blocking collectives, operate(): panel = lax.all_gather(scaled, 'row', axis=1, tiled=True)  30.3 us
    unnamed x1, blocking collectives  25.2 us
    dot_general x3, matrix products, operate(): jnp.einsum('kti,tl->kli', product, onehot, precision=lax.Precision.HIGHEST)  6.25 us
    reduce_sum x1, other arithmetic, on_device(): magnitude = jnp.sum(jnp.abs(tiles), axis=2)  5.65 us
  transfers between devices with their start and end apart: 3, of which 3 were waited for; matrix products, arithmetic and copies ran while one was open for 0% of the time, Pallas kernels for 0%

commit v1 on v0

--- a/solution.py
+++ b/solution.py
@@ -6,6 +6,19 @@
 TB = 128
 K = 32
 STEPS = 3
+
+
+def gather_around(shard, axis, dim):
+    size, index, rows = (lax.axis_size(axis), lax.axis_index(axis), shard.shape[dim])
+    upward = [(i, (i + 1) % size) for i in range(size)]
+    filled = jnp.zeros((*shard.shape[:dim], size * rows, *shard.shape[dim + 1 :]), shard.dtype)
+    held = shard
+    for step in range(size):
+        owner = (index - step) % size
+        filled = lax.dynamic_update_slice_in_dim(filled, held, owner * rows, axis=dim)
+        if step < size - 1:
+            held = lax.ppermute(held, axis, upward)
+    return filled
 
 
 def on_device(vectors, tiles, tile_row, tile_col):
@@ -29,7 +42,7 @@
 
     def operate(current):
         scaled = current * scale[None, :]
-        panel = lax.all_gather(scaled, "row", axis=1, tiled=True)
+        panel = gather_around(scaled, "row", 1)
         picked = jnp.take(panel.reshape(K, local_cols, TB), cols_here, axis=1)
         product = jnp.einsum("tij,ktj->kti", tiles, picked, precision=lax.Precision.HIGHEST)
         partial_value = jnp.einsum(

time: 276 us -> 301 us (1.091)
  waiting for transfers between devices: 90.1 us -> 127 us
  blocking collectives: 99 us -> 69.3 us
  starting transfers between devices: 0.12 us -> 20.4 us
    ppermute x0 -> x9, waiting for transfers between devices: none -> 31.6 us  [gather_around(): held = lax.ppermute(held, axis, upward)]
    all_gather x3 -> x0, blocking collectives: 30.3 us -> none  [operate(): panel = lax.all_gather(scaled, 'row', axis=1, tiled=True)]
    ppermute x0 -> x9, starting transfers between devices: none -> 20.2 us  [gather_around(): held = lax.ppermute(held, axis, upward)]
    reduce_scatter x3, waiting for transfers between devices: 90 us -> 94.9 us  [operate(): lax.psum_scatter(partial_value, 'col', scatter_dimension=1, tiled=True)]
  transfers between devices with their start and end apart: 3 -> 12, of which waited for: 3 -> 12; matrix products, arithmetic and copies ran while one was open for 0% -> 0% of each run, Pallas kernels for 0% -> 0%
where the time goes in v1:
time: 301 us
  waiting for transfers between devices  127 us (42%)
  blocking collectives  69.3 us (23%)
  matrix products  53.1 us (18%)
  starting transfers between devices  20.4 us (7%)
  between operations  14.7 us (5%)
  other arithmetic  9.11 us (3%)
  local copies, waits for them, and re-layouts  8.11 us (3%)
    reduce_scatter x3, waiting for transfers between devices, operate(): lax.psum_scatter(partial_value, 'col', scatter_dimension=1, tiled=True)  94.9 us
    dot_general x3, matrix products, operate(): jnp.einsum('tij,ktj->kti', tiles, picked, precision=lax.Precision.HIGHEST)  46.4 us
    psum x1, blocking collectives, on_device(): gram = lax.psum(local_gram, ('row', 'col')) / (width * n_row * n_col)  44 us
    ppermute x9, waiting for transfers between devices, gather_around(): held = lax.ppermute(held, axis, upward)  31.6 us
    unnamed x1, blocking collectives  25.2 us
    ppermute x9, starting transfers between devices, gather_around(): held = lax.ppermute(held, axis, upward)  20.2 us
    dot_general x3, matrix products, operate(): jnp.einsum('kti,tl->kli', product, onehot, precision=lax.Precision.HIGHEST)  6.24 us
  transfers between devices with their start and end apart: 12, of which 12 were waited for; matrix products, arithmetic and copies ran while one was open for 0% of the time, Pallas kernels for 0%

profile of v1, /device:TPU:10, one launch (start us, length us, event | category | flops | bytes accessed | tf_op | source)
XLA Modules:
  0.0 301.2 jit_solution(17734130623007926917)
XLA Ops:
  7.3 5.7 %abs_reduce_fusion = f32[128,128]{1,0:T(8,128)S(1)} fusion(f32[128,128,128]{2,1,0:T(8,128)} %param.7), kind=kLoop, calls=%fused_computation.3 | loop fusion | flops 4177920 | bytes 8454144 | tf_op jit(solution)/shard_map/reduce_sum | solution.py:36
  13.1 25.2 %all-reduce = f32[8192]{0:T(1024)S(1)} all-reduce(f32[8192]{0:T(1024)S(1)} %convolution_bitcast_fusion), channel_id=2, replica_groups=mesh['row'=4,'col'=8] {'col'}, use_global_device_ids=true, to_apply=%region_1.0.clone | all-reduce | flops 8192 | bytes 65536
  41.2 4.1 %collective-permute-done = f32[32,1024]{1,0:T(8,128)S(1)} collective-permute-done((f32[32,1024]{1,0:T(8,128)S(1)}, f32[32,1024]{1,0:T(8,128)S(1)}, u32[]{:S(2)}, u32[]{:S(2)}) %collective-permute-start) | collective-permute-done | bytes 131104 | tf_op jit(solution)/shard_map/ppermute | solution.py:20
  45.3 3.0 %collective-permute-start.1 = (f32[32,1024]{1,0:T(8,128)S(1)}, f32[32,1024]{1,0:T(8,128)S(1)}, u32[]{:S(2)}, u32[]{:S(2)}) collective-permute-start(f32[32,1024]{1,0:T(8,128)S(1)} %collective-permute-done), channel_id=1, source_target_pairs={{0,8},{8,16},{16,24},{24,0},{1,9},{9,17},{17,25},{25,1},{2,10},{10... | collective-permute-start | bytes 393224 | tf_op jit(solution)/shard_map/ppermute | solution.py:20
  48.4 3.0 %collective-permute-done.1 = f32[32,1024]{1,0:T(8,128)S(1)} collective-permute-done((f32[32,1024]{1,0:T(8,128)S(1)}, f32[32,1024]{1,0:T(8,128)S(1)}, u32[]{:S(2)}, u32[]{:S(2)}) %collective-permute-start.1) | collective-permute-done | bytes 131104 | tf_op jit(solution)/shard_map/ppermute | solution.py:20
  51.4 3.4 %collective-permute-start.2 = (f32[32,1024]{1,0:T(8,128)S(1)}, f32[32,1024]{1,0:T(8,128)S(1)}, u32[]{:S(2)}, u32[]{:S(2)}) collective-permute-start(f32[32,1024]{1,0:T(8,128)S(1)} %collective-permute-done.1), channel_id=1, source_target_pairs={{0,8},{8,16},{16,24},{24,0},{1,9},{9,17},{17,25},{25,1},{2,10},{10... | collective-permute-start | bytes 393224 | tf_op jit(solution)/shard_map/ppermute | solution.py:20
  54.8 2.5 collective-permute-done.2
  58.2 15.5 %fusion.15 = f32[32,128,128]{2,0,1:T(8,128)S(1)} fusion(f32[128,128,128]{2,1,0:T(8,128)} %param.7, f32[128,32,128]{2,1,0:T(8,128)S(1)} %gather_fusion, pred[128]{0:T(512)(128)(4,1)S(1)} %compare_and_fusion), kind=kOutput, calls=%fused_computation.19 | convolution fusion | flops 805830656 | bytes 12583040 | tf_op jit(solution)/shard_map/tij,ktj->kti/dot_general | solution.py:47
  77.4 31.6 %reduce-scatter.4.cloned.1.call-done = f32[32,1024]{1,0:T(8,128)} async-done(((f32[32,8192]{1,0:T(8,128)}), f32[32,1024]{1,0:T(8,128)}) %reduce-scatter.4.cloned.1.call-update) | async-done | bytes 131088 | tf_op jit(solution)/shard_map/reduce_scatter | solution.py:51
  111.4 4.7 %collective-permute-done.3 = f32[32,1024]{1,0:T(8,128)S(1)} collective-permute-done((f32[32,1024]{1,0:T(8,128)S(1)}, f32[32,1024]{1,0:T(8,128)S(1)}, u32[]{:S(2)}, u32[]{:S(2)}) %collective-permute-start.3) | collective-permute-done | bytes 131104 | tf_op jit(solution)/shard_map/ppermute | solution.py:20
  118.0 3.5 %collective-permute-done.4 = f32[32,1024]{1,0:T(8,128)S(1)} collective-permute-done((f32[32,1024]{1,0:T(8,128)S(1)}, f32[32,1024]{1,0:T(8,128)S(1)}, u32[]{:S(2)}, u32[]{:S(2)}) %collective-permute-start.4) | collective-permute-done | bytes 131104 | tf_op jit(solution)/shard_map/ppermute | solution.py:20
  121.5 3.3 %collective-permute-start.5 = (f32[32,1024]{1,0:T(8,128)S(1)}, f32[32,1024]{1,0:T(8,128)S(1)}, u32[]{:S(2)}, u32[]{:S(2)}) collective-permute-start(f32[32,1024]{1,0:T(8,128)S(1)} %collective-permute-done.4), channel_id=1, source_target_pairs={{0,8},{8,16},{16,24},{24,0},{1,9},{9,17},{17,25},{25,1},{2,10},{10... | collective-permute-start | bytes 393224 | tf_op jit(solution)/shard_map/ppermute | solution.py:20
  124.9 2.5 collective-permute-done.5
  128.2 15.5 %fusion.18 = f32[32,128,128]{2,0,1:T(8,128)S(1)} fusion(f32[128,128,128]{2,1,0:T(8,128)} %param.7, f32[128,32,128]{2,1,0:T(8,128)S(1)} %gather_fusion.1, pred[128]{0:T(512)(128)(4,1)S(1)} %compare_and_fusion), kind=kOutput, calls=%fused_computation.20 | convolution fusion | flops 805830656 | bytes 12583040 | tf_op jit(solution)/shard_map/tij,ktj->kti/dot_general | solution.py:47
  143.7 2.1 fusion.8
  147.5 31.7 %reduce-scatter.6.cloned.1.call-done = f32[32,1024]{1,0:T(8,128)} async-done(((f32[32,8192]{1,0:T(8,128)}), f32[32,1024]{1,0:T(8,128)}) %reduce-scatter.6.cloned.1.call-update) | async-done | bytes 131088 | tf_op jit(solution)/shard_map/reduce_scatter | solution.py:51
  181.3 4.9 %collective-permute-done.6 = f32[32,1024]{1,0:T(8,128)S(1)} collective-permute-done((f32[32,1024]{1,0:T(8,128)S(1)}, f32[32,1024]{1,0:T(8,128)S(1)}, u32[]{:S(2)}, u32[]{:S(2)}) %collective-permute-start.6) | collective-permute-done | bytes 131104 | tf_op jit(solution)/shard_map/ppermute | solution.py:20
  187.5 3.9 %collective-permute-done.7 = f32[32,1024]{1,0:T(8,128)S(1)} collective-permute-done((f32[32,1024]{1,0:T(8,128)S(1)}, f32[32,1024]{1,0:T(8,128)S(1)}, u32[]{:S(2)}, u32[]{:S(2)}) %collective-permute-start.7) | collective-permute-done | bytes 131104 | tf_op jit(solution)/shard_map/ppermute | solution.py:20
  191.4 3.3 %collective-permute-start.8 = (f32[32,1024]{1,0:T(8,128)S(1)}, f32[32,1024]{1,0:T(8,128)S(1)}, u32[]{:S(2)}, u32[]{:S(2)}) collective-permute-start(f32[32,1024]{1,0:T(8,128)S(1)} %collective-permute-done.7), channel_id=1, source_target_pairs={{0,8},{8,16},{16,24},{24,0},{1,9},{9,17},{17,25},{25,1},{2,10},{10... | collective-permute-start | bytes 393224 | tf_op jit(solution)/shard_map/ppermute | solution.py:20
  194.7 2.5 collective-permute-done.8
  198.0 15.5 %fusion.21 = f32[32,128,128]{2,0,1:T(8,128)S(1)} fusion(f32[128,128,128]{2,1,0:T(8,128)} %param.7, f32[128,32,128]{2,1,0:T(8,128)S(1)} %gather_fusion.2, pred[128]{0:T(512)(128)(4,1)S(1)} %compare_and_fusion), kind=kOutput, calls=%fused_computation.21 | convolution fusion | flops 805830656 | bytes 12583040 | tf_op jit(solution)/shard_map/tij,ktj->kti/dot_general | solution.py:47
  213.5 2.1 fusion.6
  217.2 31.6 %reduce-scatter.8.cloned.1.call-done = f32[32,1024]{1,0:T(8,128)} async-done(((f32[32,8192]{1,0:T(8,128)}), f32[32,1024]{1,0:T(8,128)}) %reduce-scatter.8.cloned.1.call-update) | async-done | bytes 131088 | tf_op jit(solution)/shard_map/reduce_scatter | solution.py:51
  250.0 44.0 %psum.7 = f32[32,32]{1,0:T(8,128)S(1)} all-reduce(f32[32,32]{1,0:T(8,128)S(1)} %fusion.42), channel_id=1, replica_groups=mesh['row'=4,'col'=8] {'row','col'}, use_global_device_ids=true, to_apply=%region_5.7 | all-reduce | flops 1024 | bytes 8192 | tf_op jit(solution)/shard_map/psum | solution.py:61
  (57 shorter events, 21.4 us)
Async XLA Ops:
  7.2 101.8 %reduce-scatter.4.cloned.1.call-start = ((), (), s32[]{:S(2)}) async-start(), calls=%async_computation.3 | async-start | bytes 1179648 | tf_op jit(solution)/shard_map/reduce_scatter | solution.py:51
  7.2 5.7 %copy-start.3 = (s32[1,128]{1,0:T(1,128)S(1)}, s32[1,128]{1,0:T(1,128)}, u32[]{:S(2)}) copy-start(s32[1,128]{1,0:T(1,128)} %param.8) | copy-start | bytes 1540
  7.2 31.1 %copy-start.5 = (u32[32]{0:T(128)S(1)}, u32[32]{0:T(128)}, u32[]{:S(2)}) copy-start(u32[32]{0:T(128)} %constant.84) | copy-start | bytes 388
  7.3 32.4 %copy-start.1 = (f32[32,1024]{1,0:T(8,128)S(1)}, f32[32,1024]{1,0:T(8,128)}, u32[]{:S(2)}) copy-start(f32[32,1024]{1,0:T(8,128)} %param.6) | copy-start | bytes 393220
  7.3 34.0 %copy-start.4 = (s32[1,128]{1,0:T(1,128)S(1)}, s32[1,128]{1,0:T(1,128)}, u32[]{:S(2)}) copy-start(s32[1,128]{1,0:T(1,128)} %param.9) | copy-start | bytes 1540
  39.7 5.7 %collective-permute-start = (f32[32,1024]{1,0:T(8,128)S(1)}, f32[32,1024]{1,0:T(8,128)S(1)}, u32[]{:S(2)}, u32[]{:S(2)}) collective-permute-start(f32[32,1024]{1,0:T(8,128)S(1)} %get-tuple-element.8), channel_id=1, source_target_pairs={{0,8},{8,16},{16,24},{24,0},{1,9},{9,17},{17,25},{25,1},{2,10},{10... | collective-permute-start | bytes 393224 | tf_op jit(solution)/shard_map/ppermute | solution.py:20
  45.3 6.1 %collective-permute-start.1 = (f32[32,1024]{1,0:T(8,128)S(1)}, f32[32,1024]{1,0:T(8,128)S(1)}, u32[]{:S(2)}, u32[]{:S(2)}) collective-permute-start(f32[32,1024]{1,0:T(8,128)S(1)} %collective-permute-done), channel_id=1, source_target_pairs={{0,8},{8,16},{16,24},{24,0},{1,9},{9,17},{17,25},{25,1},{2,10},{10... | collective-permute-start | bytes 393224 | tf_op jit(solution)/shard_map/ppermute | solution.py:20
  51.4 5.9 %collective-permute-start.2 = (f32[32,1024]{1,0:T(8,128)S(1)}, f32[32,1024]{1,0:T(8,128)S(1)}, u32[]{:S(2)}, u32[]{:S(2)}) collective-permute-start(f32[32,1024]{1,0:T(8,128)S(1)} %collective-permute-done.1), channel_id=1, source_target_pairs={{0,8},{8,16},{16,24},{24,0},{1,9},{9,17},{17,25},{25,1},{2,10},{10... | collective-permute-start | bytes 393224 | tf_op jit(solution)/shard_map/ppermute | solution.py:20
  77.3 101.9 %reduce-scatter.6.cloned.1.call-start = ((), (), s32[]{:S(2)}) async-start(), calls=%async_computation.4 | async-start | bytes 1179648 | tf_op jit(solution)/shard_map/reduce_scatter | solution.py:51
  109.9 6.2 %collective-permute-start.3 = (f32[32,1024]{1,0:T(8,128)S(1)}, f32[32,1024]{1,0:T(8,128)S(1)}, u32[]{:S(2)}, u32[]{:S(2)}) collective-permute-start(f32[32,1024]{1,0:T(8,128)S(1)} %get-tuple-element.6), channel_id=1, source_target_pairs={{0,8},{8,16},{16,24},{24,0},{1,9},{9,17},{17,25},{25,1},{2,10},{10... | collective-permute-start | bytes 393224 | tf_op jit(solution)/shard_map/ppermute | solution.py:20
  116.2 5.3 %collective-permute-start.4 = (f32[32,1024]{1,0:T(8,128)S(1)}, f32[32,1024]{1,0:T(8,128)S(1)}, u32[]{:S(2)}, u32[]{:S(2)}) collective-permute-start(f32[32,1024]{1,0:T(8,128)S(1)} %collective-permute-done.3), channel_id=1, source_target_pairs={{0,8},{8,16},{16,24},{24,0},{1,9},{9,17},{17,25},{25,1},{2,10},{10... | collective-permute-start | bytes 393224 | tf_op jit(solution)/shard_map/ppermute | solution.py:20
  121.5 5.9 %collective-permute-start.5 = (f32[32,1024]{1,0:T(8,128)S(1)}, f32[32,1024]{1,0:T(8,128)S(1)}, u32[]{:S(2)}, u32[]{:S(2)}) collective-permute-start(f32[32,1024]{1,0:T(8,128)S(1)} %collective-permute-done.4), channel_id=1, source_target_pairs={{0,8},{8,16},{16,24},{24,0},{1,9},{9,17},{17,25},{25,1},{2,10},{10... | collective-permute-start | bytes 393224 | tf_op jit(solution)/shard_map/ppermute | solution.py:20
  147.4 101.4 %reduce-scatter.8.cloned.1.call-start = ((), (), s32[]{:S(2)}) async-start(), calls=%async_computation.5 | async-start | bytes 1179648 | tf_op jit(solution)/shard_map/reduce_scatter | solution.py:51
  180.2 6.0 %collective-permute-start.6 = (f32[32,1024]{1,0:T(8,128)S(1)}, f32[32,1024]{1,0:T(8,128)S(1)}, u32[]{:S(2)}, u32[]{:S(2)}) collective-permute-start(f32[32,1024]{1,0:T(8,128)S(1)} %get-tuple-element.4), channel_id=1, source_target_pairs={{0,8},{8,16},{16,24},{24,0},{1,9},{9,17},{17,25},{25,1},{2,10},{10... | collective-permute-start | bytes 393224 | tf_op jit(solution)/shard_map/ppermute | solution.py:20
  186.2 5.2 %collective-permute-start.7 = (f32[32,1024]{1,0:T(8,128)S(1)}, f32[32,1024]{1,0:T(8,128)S(1)}, u32[]{:S(2)}, u32[]{:S(2)}) collective-permute-start(f32[32,1024]{1,0:T(8,128)S(1)} %collective-permute-done.6), channel_id=1, source_target_pairs={{0,8},{8,16},{16,24},{24,0},{1,9},{9,17},{17,25},{25,1},{2,10},{10... | collective-permute-start | bytes 393224 | tf_op jit(solution)/shard_map/ppermute | solution.py:20
  191.4 5.8 %collective-permute-start.8 = (f32[32,1024]{1,0:T(8,128)S(1)}, f32[32,1024]{1,0:T(8,128)S(1)}, u32[]{:S(2)}, u32[]{:S(2)}) collective-permute-start(f32[32,1024]{1,0:T(8,128)S(1)} %collective-permute-done.7), channel_id=1, source_target_pairs={{0,8},{8,16},{16,24},{24,0},{1,9},{9,17},{17,25},{25,1},{2,10},{10... | collective-permute-start | bytes 393224 | tf_op jit(solution)/shard_map/ppermute | solution.py:20
  215.6 33.2 %copy-start.2 = (f32[32,1024]{1,0:T(8,128)S(1)}, f32[32,1024]{1,0:T(8,128)}, u32[]{:S(2)}) copy-start(f32[32,1024]{1,0:T(8,128)} %reduce-scatter.4.cloned.1.call-done) | copy-start | bytes 393220
  249.7 44.9 %copy-start = (f32[32,1024]{1,0:T(8,128)}, f32[32,1024]{1,0:T(8,128)S(1)}, u32[]{:S(2)}) copy-start(f32[32,1024]{1,0:T(8,128)S(1)} %multiply_subtract_fusion) | copy-start | bytes 393220
Sparse Core Ops, SparseCore 0:
  77.5 31.4 reduce-scatter.3
  147.5 31.6 reduce-scatter.5
  217.4 31.4 reduce-scatter.7
